TPU v7x, 128 devices: a whole 4x4x4 slice. The times are simulated.
128 devices in a mesh: blk: 8 (over x_lo, y), head: 8 (over z, core), grp: 2 (over x_hi).
Axes of the slice: x: 4 (x_hi: 2, x_lo: 2; x = x_hi * 2 + x_lo), y: 4, z: 4, core: 2. Of those that a mesh axis runs over, the one named last changes fastest.
Arguments:
- t_query: bfloat16 [8192, 4096], P('blk', ('head', 'grp')), may hold values from -80 to 80
- t_key: bfloat16 [8192, 4096], P('blk', ('head', 'grp')), may hold values from -80 to 80
- t_value: bfloat16 [8192, 4096], P('blk', ('head', 'grp')), may hold values from -6 to 6
- t_out: bfloat16 [4096, 4096], P(('head', 'grp')), may hold values from -0.09375 to 0.09375
- s_query: bfloat16 [8192, 2048], P('blk', ('head', 'grp')), may hold values from -80 to 80
- s_key: bfloat16 [8192, 2048], P('blk', ('head', 'grp')), may hold values from -80 to 80
- s_value: bfloat16 [8192, 2048], P('blk', ('head', 'grp')), may hold values from -6 to 6
- s_out: bfloat16 [2048, 4096], P(('head', 'grp')), may hold values from -0.125 to 0.125
- segments: int32 [8192], P('blk'), may hold values from 0 to 1, never falling along the last dimension, each value on 1 to 8128 neighbouring positions
- selection: int32 [128, 16], P('blk'), may hold values from 0 to 127, as said below
Outputs:
- mismatch: float32 [8192, 4096], P('blk', ('head', 'grp'))
- s_dq: float32 [8192, 2048], P('blk', ('head', 'grp'))
- s_dk: float32 [8192, 2048], P('blk', ('head', 'grp'))
- s_dv: float32 [8192, 2048], P('blk', ('head', 'grp'))
Inputs may be any that keep to these rules, and one draw needn't show every extreme that they name: `selection`: entry 0 of row b is b itself; for b >= 64, entry 1 of row b is b - 64; every entry of row b lies between 0 and b; entries of a row may repeat. `segments`: document numbers never fall along the sequence.
All inputs are finite; a program needn't handle non-finite values.
Results may differ from a plain program's by a relative error of at most 0.015.
Values may be sent and summed in bfloat16 or wider, within the bound.
No kernel may reach another device: no remote copies, remote signals or barrier semaphores. Data moves between devices by JAX's collectives and lax.ppermute only.
A program may use at most 128 MiB of HBM per device.

v0:
```python
import math
import jax
import jax.numpy as jnp
from jax import lax
from jax.sharding import PartitionSpec as P

HD = 128
BS = 64
NSEL = 16
masked_score = -1e30


def student_forward(queries, key_all, value_all, segment_all, selection, first_row):
    row_count = queries.shape[0]
    head_count = queries.shape[1] // HD
    blocks = row_count // BS
    query_blocks = queries.reshape(blocks, BS, head_count, HD)
    key_blocks = key_all.reshape(-1, BS, head_count, HD)[selection].reshape(
        blocks, NSEL * BS, head_count, HD
    )
    value_blocks = value_all.reshape(-1, BS, head_count, HD)[selection].reshape(
        blocks, NSEL * BS, head_count, HD
    )
    key_pos = (selection[:, :, None] * BS + jnp.arange(BS)[None, None, :]).reshape(
        blocks, NSEL * BS
    )
    query_pos = (first_row + jnp.arange(row_count)).reshape(blocks, BS)
    key_seg = segment_all[key_pos]
    query_seg = segment_all[query_pos]
    scores = jnp.einsum(
        "bqhd,bkhd->bhqk", query_blocks, key_blocks, preferred_element_type=jnp.float32
    ) * HD ** (-0.5)
    allowed = (
        (key_pos[:, None, :] <= query_pos[:, :, None])
        & (key_seg[:, None, :] == query_seg[:, :, None])
    )[:, None]
    scores = jnp.where(allowed, scores, masked_score)
    largest = jnp.max(scores, axis=3, keepdims=True)
    weights = jnp.where(allowed, jnp.exp(scores - largest), 0.0)
    weights = weights / jnp.sum(weights, axis=3, keepdims=True)
    value_wide = value_blocks.astype(jnp.float32)
    blended = jnp.einsum("bhqk,bkhd->bqhd", weights, value_wide, precision=lax.Precision.HIGHEST)
    saved = (query_blocks, key_blocks, value_wide, weights, blended)
    return (blended.reshape(row_count, head_count * HD), saved)


def student_backward(grad_attn, saved, selection, token_count):
    query_blocks, key_blocks, value_wide, weights, blended = saved
    blocks, _, head_count, _ = query_blocks.shape
    row_count = blocks * BS
    grad_blocks = grad_attn.reshape(blocks, BS, head_count, HD)
    value_grad = jnp.einsum(
        "bhqk,bqhd->bkhd", weights, grad_blocks, precision=lax.Precision.HIGHEST
    )
    weight_grad = jnp.einsum(
        "bqhd,bkhd->bhqk", grad_blocks, value_wide, precision=lax.Precision.HIGHEST
    )
    row_dots = jnp.sum(grad_blocks * blended, axis=3).transpose(0, 2, 1)[..., None]
    score_grad = weights * (weight_grad - row_dots) * HD ** (-0.5)
    query_grad = jnp.einsum(
        "bhqk,bkhd->bqhd",
        score_grad,
        key_blocks.astype(jnp.float32),
        precision=lax.Precision.HIGHEST,
    )
    key_grad = jnp.einsum(
        "bhqk,bqhd->bkhd",
        score_grad,
        query_blocks.astype(jnp.float32),
        precision=lax.Precision.HIGHEST,
    )
    flat_sel = selection.reshape(-1)
    width = head_count * HD
    key_total = (
        jnp.zeros((token_count // BS, BS, width), jnp.float32)
        .at[flat_sel]
        .add(key_grad.reshape(blocks * NSEL, BS, width))
    )
    value_total = (
        jnp.zeros((token_count // BS, BS, width), jnp.float32)
        .at[flat_sel]
        .add(value_grad.reshape(blocks * NSEL, BS, width))
    )
    return (
        query_grad.reshape(row_count, width),
        key_total.reshape(token_count, width),
        value_total.reshape(token_count, width),
    )


def teacher_update(
    carried, key_rows, value_rows, seg_rows, first_key, queries, query_seg, query_pos
):
    running_max, running_sum, weighted = carried
    head_count = queries.shape[1]
    key_heads = key_rows.reshape(key_rows.shape[0], head_count, HD)
    value_heads = value_rows.reshape(value_rows.shape[0], head_count, HD)
    scores = jnp.einsum(
        "qhd,khd->hqk", queries, key_heads, preferred_element_type=jnp.float32
    ) * HD ** (-0.5)
    key_pos = first_key + jnp.arange(key_rows.shape[0])
    allowed = (
        (key_pos[None, :] <= query_pos[:, None]) & (seg_rows[None, :] == query_seg[:, None])
    )[None]
    scores = jnp.where(allowed, scores, masked_score)
    new_max = jnp.maximum(running_max, jnp.max(scores, axis=2))
    factor = jnp.exp(running_max - new_max)
    weights = jnp.where(allowed, jnp.exp(scores - new_max[..., None]), 0.0)
    running_sum = factor * running_sum + jnp.sum(weights, axis=2)
    product = jnp.einsum(
        "hqk,khd->hqd",
        weights.astype(jnp.bfloat16),
        value_heads,
        preferred_element_type=jnp.float32,
    )
    weighted = factor[..., None] * weighted + product
    return (new_max, running_sum, weighted)


def teacher_fold(carried, key_rows, value_rows, seg_rows, queries, query_seg, query_pos):
    piece_rows = key_rows.shape[0]
    block_rows = math.gcd(piece_rows, 512)
    turn_count = piece_rows // block_rows
    last_query = query_pos[-1]

    def one_turn(turn_index, status):
        offset = turn_index * block_rows
        key_block = lax.dynamic_slice_in_dim(key_rows, offset, block_rows, 0)
        value_block = lax.dynamic_slice_in_dim(value_rows, offset, block_rows, 0)
        seg_block = lax.dynamic_slice_in_dim(seg_rows, offset, block_rows, 0)

        def compute(inner):
            return teacher_update(
                inner, key_block, value_block, seg_block, offset, queries, query_seg, query_pos
            )

        def keep(inner):
            return inner

        return lax.cond(offset > last_query, keep, compute, status)

    return lax.fori_loop(0, turn_count, one_turn, carried)


def on_device(t_query, t_key, t_value, t_out, s_query, s_key, s_value, s_out, segments, selection):
    row_count = t_query.shape[0]
    head_count = t_query.shape[1] // HD
    cycle_size = lax.axis_size("blk")
    my_index = lax.axis_index("blk")
    first_row = my_index * row_count
    token_count = row_count * cycle_size
    query_pos = first_row + jnp.arange(row_count)
    queries = t_query.reshape(row_count, head_count, HD)
    initial = (
        jnp.full((head_count, row_count), masked_score, jnp.float32),
        jnp.zeros((head_count, row_count), jnp.float32),
        jnp.zeros((head_count, row_count, HD), jnp.float32),
    )
    teacher_state = teacher_fold(
        initial,
        lax.all_gather(t_key, "blk", axis=0, tiled=True),
        lax.all_gather(t_value, "blk", axis=0, tiled=True),
        lax.all_gather(segments, "blk", axis=0, tiled=True),
        queries,
        segments,
        query_pos,
    )
    key_full, value_full, seg_full = (
        lax.all_gather(s_key, "blk", axis=0, tiled=True),
        lax.all_gather(s_value, "blk", axis=0, tiled=True),
        lax.all_gather(segments, "blk", axis=0, tiled=True),
    )
    t_attn = (
        (teacher_state[2] / teacher_state[1][..., None])
        .transpose(1, 0, 2)
        .reshape(row_count, head_count * HD)
    )
    t_attn = t_attn.astype(jnp.bfloat16)
    student_full, saved = student_forward(
        s_query, key_full, value_full, seg_full, selection, first_row
    )
    s_attn = student_full.astype(jnp.bfloat16)
    partial_terms = jnp.dot(s_attn, s_out, preferred_element_type=jnp.float32) - jnp.dot(
        t_attn, t_out, preferred_element_type=jnp.float32
    )
    contract = (((1,), (1,)), ((), ()))
    mismatch = lax.psum_scatter(
        partial_terms.astype(jnp.bfloat16), ("head", "grp"), scatter_dimension=1, tiled=True
    ).astype(jnp.float32)
    grad_attn = lax.dot_general(
        lax.all_gather(mismatch.astype(jnp.bfloat16), ("head", "grp"), axis=1, tiled=True),
        s_out,
        contract,
        preferred_element_type=jnp.float32,
    )
    grad_query, grad_keys, grad_values = student_backward(grad_attn, saved, selection, token_count)
    key_grads, value_grads = (
        lax.psum_scatter(
            grad_keys.astype(jnp.bfloat16), "blk", scatter_dimension=0, tiled=True
        ).astype(jnp.float32),
        lax.psum_scatter(
            grad_values.astype(jnp.bfloat16), "blk", scatter_dimension=0, tiled=True
        ).astype(jnp.float32),
    )
    return (mismatch, grad_query, key_grads, value_grads)


def solution(mesh):
    in_specs = (
        P("blk", ("head", "grp")),
        P("blk", ("head", "grp")),
        P("blk", ("head", "grp")),
        P(("head", "grp"), None),
        P("blk", ("head", "grp")),
        P("blk", ("head", "grp")),
        P("blk", ("head", "grp")),
        P(("head", "grp"), None),
        P("blk"),
        P("blk", None),
    )
    out_specs = (
        P("blk", ("head", "grp")),
        P("blk", ("head", "grp")),
        P("blk", ("head", "grp")),
        P("blk", ("head", "grp")),
    )
    return jax.shard_map(
        on_device, mesh=mesh, in_specs=in_specs, out_specs=out_specs, check_vma=False
    )
```

profile of v0, /device:TPU:0, one launch (start us, length us, event | category | flops | bytes accessed | tf_op | source)
XLA Modules:
  0.0 699.5 jit_solution(14955056844412528402)
XLA Ops:
  7.2 0.7 all-gather.6.cloned.1.call-update
  8.0 0.7 all-gather.8.cloned.1.call-update
  8.7 2.0 copy.27
  10.8 2.0 copy.29
  13.0 0.7 broadcast_multiply_fusion
  14.1 28.7 %all_gather.20 = s32[8192]{0:T(1024)S(1)} all-gather(s32[1024]{0:T(1024)S(1)} %copy-done.12), channel_id=1, replica_groups=mesh['blk'=8,'head'=8,'grp'=2] {'blk'}, dimensions={0}, use_global_device_ids=true | all-gather | bytes 36864 | tf_op jit(solution)/shard_map/all_gather | solution.py:171
  42.8 6.1 gather_fusion.2
  49.2 90.5 %gather_fusion.1 = s32[16384]{0:T(1024)S(1)} fusion(s32[8192]{0:T(1024)S(1)} %all_gather.20, s32[16384]{0:T(1024)S(1)} %broadcast_clamp_fusion), kind=kCustom, calls=%fused_computation.1 | custom fusion | bytes 196608 | tf_op jit(solution)/shard_map/gather | solution.py:28
  141.0 4.8 gather_fusion
  145.8 4.7 gather_fusion.3
  150.5 6.2 fusion.27
  156.7 6.7 fusion.28
  163.3 8.1 %fusion.29 = f32[1024,4096]{1,0:T(8,128)} fusion(bf16[1024,128]{1,0:T(8,128)(2,1)S(1)} %bitcast.102, bf16[128,4096]{1,0:T(8,128)(2,1)S(1)} %copy-done.7), kind=kOutput, calls=%fused_computation.60 | convolution fusion | flops 1073741824 | bytes 18087936 | tf_op jit(solution)/shard_map/dot_general | solution.py:183
  171.4 32.4 %all-gather.12.cloned.1.call-done = bf16[8192,256]{0,1:T(8,128)(2,1)} async-done(((bf16[1024,256]{0,1:T(8,128)(2,1)}), bf16[8192,256]{0,1:T(8,128)(2,1)}) %all-gather.12.cloned.1.call-update) | async-done | bytes 4194320 | tf_op jit(solution)/shard_map/all_gather | solution.py:162
  203.9 1.0 broadcast_in_dim.72
  204.9 25.1 %while.18 = (s32[]{:T(128)}, f32[2,1024]{1,0:T(2,128)S(1)}, f32[2,1024]{1,0:T(2,128)S(1)}, f32[2,1024,128]{2,1,0:T(8,128)}, s32[]{:T(128)}, /*index=5*/s32[8192]...) while((s32[]{:T(128)}, f32[2,1024]{1,0:T(2,128)S(1)}, ...), condition=%wide.region_7.8_spmd.clone, body=%wide.region_2.7_spmd.clone.sunk | while | flops 552605184 | bytes 27425168 | solution.py:142
  205.5 7.0 conditional.3
  206.2 1.1 constant_dynamic-slice_fusion
  207.2 1.1 fusion.2
  208.4 1.1 fusion.4
  209.5 2.0 fusion.8
  211.5 1.0 copy-done.5
  213.1 7.0 conditional.3
  213.8 1.1 constant_dynamic-slice_fusion
  214.8 1.1 fusion.2
  216.0 1.1 fusion.4
  217.1 2.0 fusion.8
  219.1 1.0 copy-done.5
  230.0 1.6 copy.31
  231.7 11.4 %subtract_convert_fusion = bf16[1024,4096]{1,0:T(8,128)(2,1)} fusion(f32[1024,4096]{1,0:T(8,128)} %fusion.29, bf16[1024,256]{0,1:T(8,128)(2,1)S(1)} %bitcast.96, bf16[256,4096]{1,0:T(8,128)(2,1)S(1)} %copy-done), kind=kOutput, calls=%fused_computation.26 | convolution fusion | flops 2155872256 | bytes 27787264 | tf_op jit(solution)/shard_map/dot_general | solution.py:183
  243.2 197.5 %reduce-scatter.4.cloned.1.call-done = bf16[1024,256]{1,0:T(8,128)(2,1)} async-done(((bf16[1024,4096]{1,0:T(8,128)(2,1)}), bf16[1024,256]{1,0:T(8,128)(2,1)}) %reduce-scatter.4.cloned.1.call-update) | async-done | bytes 524304 | tf_op jit(solution)/shard_map/reduce_scatter | solution.py:187
  441.1 77.8 %all-gather.14.cloned.1.call-done = bf16[1024,4096]{1,0:T(8,128)(2,1)} async-done(((bf16[1024,256]{1,0:T(8,128)(2,1)}), bf16[1024,4096]{1,0:T(8,128)(2,1)}) %all-gather.14.cloned.1.call-update) | async-done | bytes 8388624 | tf_op jit(solution)/shard_map/all_gather | solution.py:191
  518.8 5.9 fusion.30
  525.0 4.6 multiply_multiply_fusion
  529.6 9.0 %fusion.32 = f32[16,1024,128]{2,1,0:T(8,128)} fusion(f32[16,64,1024]{2,1,0:T(8,128)S(1)} %multiply_multiply_fusion, bf16[16,64,128]{2,1,0:T(8,128)(2,1)S(1)} %bitcast.104), kind=kOutput, calls=%fused_computation.63 | convolution fusion | flops 1610612736 | bytes 12845056 | tf_op jit(solution)/shard_map/bhqk,bqhd->bkhd/dot_general | solution.py:66
  538.5 2.5 broadcast.200.clone
  541.0 39.0 %scatter_fusion = f32[128,64,128]{2,1,0:T(8,128)} fusion(f32[128,64,128]{2,1,0:T(8,128)} %broadcast.200.clone, s32[256]{0:T(256)S(1)} %bitcast.106, f32[256,64,128]{2,1,0:T(8,128)} %bitcast.85), kind=kCustom, calls=%fused_computation.4 | custom fusion | flops 2097152 | bytes 25166848 | tf_op jit(solution)/shard_map/scatter-add | solution.py:77
  580.1 4.0 convert_element_type.63
  584.4 10.6 %convolution_bitcast_fusion = f32[16,1024,1,128]{1,3,0,2:T(8,128)} fusion(f32[16,64,128]{2,1,0:T(8,128)S(1)} %bitcast.101, f32[16,64,1024]{2,1,0:T(8,128)} %get-tuple-element.409, f32[16,64]{1,0:T(8,128)S(1)} %get-tuple-element.408), kind=kOutput, calls=%fused_computation.31 | convolution fusion | flops 1611661312 | bytes 13111296 | tf_op jit(solution)/shard_map/bhqk,bqhd->bkhd/dot_general | solution.py:52
  595.0 9.3 %copy.32 = f32[16,1024,1,128]{3,1,0,2:T(8,128)} copy(f32[16,1024,1,128]{1,3,0,2:T(8,128)} %convolution_bitcast_fusion) | data formatting | bytes 16777216 | tf_op jit(solution)/shard_map/bhqk,bqhd->bkhd/transpose | solution.py:52
  604.3 2.5 broadcast.200.clone.1
  606.8 39.1 %scatter_fusion.1 = f32[128,64,128]{2,1,0:T(8,128)} fusion(f32[128,64,128]{2,1,0:T(8,128)} %broadcast.200.clone.1, s32[256]{0:T(256)S(1)} %bitcast.107, f32[256,64,128]{2,1,0:T(8,128)} %bitcast.84), kind=kCustom, calls=%fused_computation.5 | custom fusion | flops 2097152 | bytes 25166848 | tf_op jit(solution)/shard_map/scatter-add | solution.py:82
  645.9 4.1 convert_element_type.66
  650.0 1.0 convert_element_type.62
  651.1 6.4 fusion.31
  657.5 1.8 convert_element_type.65
  659.2 31.6 %reduce-scatter.8.cloned.1.call-done = bf16[1024,128]{1,0:T(8,128)(2,1)} async-done(((bf16[8192,128]{1,0:T(8,128)(2,1)}), bf16[1024,128]{1,0:T(8,128)(2,1)}) %reduce-scatter.8.cloned.1.call-update) | async-done | bytes 262160 | tf_op jit(solution)/shard_map/reduce_scatter | solution.py:201
  690.8 1.8 convert_element_type.68
  (149 shorter events, 5.0 us)
Async XLA Ops:
  7.2 224.5 %copy-start = (bf16[256,4096]{1,0:T(8,128)(2,1)S(1)}, bf16[256,4096]{1,0:T(8,128)(2,1)}, u32[]{:S(2)}) copy-start(bf16[256,4096]{1,0:T(8,128)(2,1)} %param.17) | copy-start | bytes 6291460
  7.2 6.9 copy-start.12
  7.2 133.8 %all-gather.6.cloned.1.call-start = ((), (), s32[]{:S(2)}) async-start(), calls=%async_computation.3 | async-start | bytes 2359296 | tf_op jit(solution)/shard_map/all_gather | solution.py:170
  7.9 137.8 %all-gather.8.cloned.1.call-start = ((), (), s32[]{:S(2)}) async-start(), calls=%async_computation.4 | async-start | bytes 2359296 | tf_op jit(solution)/shard_map/all_gather | solution.py:169
  8.7 162.7 %all-gather.10.cloned.1.call-start = ((), (), s32[]{:S(2)}) async-start(), calls=%async_computation.5 | async-start | bytes 4718592 | tf_op jit(solution)/shard_map/all_gather | solution.py:161
  10.8 193.1 %all-gather.12.cloned.1.call-start = ((), (), s32[]{:S(2)}) async-start(), calls=%async_computation.6 | async-start | bytes 4718592 | tf_op jit(solution)/shard_map/all_gather | solution.py:162
  12.9 427.8 %reduce-scatter.4.cloned.1.call-start = ((), (), s32[]{:S(2)}) async-start(), calls=%async_computation.7 | async-start | bytes 8912896 | tf_op jit(solution)/shard_map/reduce_scatter | solution.py:187
  49.2 91.2 %copy-start.9 = (bf16[1024,256]{1,0:T(8,128)(2,1)S(1)}, bf16[1024,256]{1,0:T(8,128)(2,1)}, u32[]{:S(2)}) copy-start(bf16[1024,256]{1,0:T(8,128)(2,1)} %param.14) | copy-start | bytes 1572868
  145.8 4.7 copy-start.11
  156.7 6.7 copy-start.7
  207.2 2.3 copy-start.4
  211.5 1.0 copy-start.5
  214.8 2.3 copy-start.4
  219.1 1.0 copy-start.5
  243.1 197.8 %copy-start.13 = (s32[16,16]{1,0:T(8,128)S(1)}, s32[16,16]{1,0:T(8,128)}, u32[]{:S(2)}) copy-start(s32[16,16]{1,0:T(8,128)} %param.23) | copy-start | bytes 3076
  243.1 275.7 %copy-start.8 = (bf16[128,4096]{1,0:T(8,128)(2,1)S(1)}, bf16[128,4096]{1,0:T(8,128)(2,1)}, u32[]{:S(2)}) copy-start(bf16[128,4096]{1,0:T(8,128)(2,1)} %param.21) | copy-start | bytes 3145732
  243.1 275.7 %all-gather.14.cloned.1.call-start = ((), (), s32[]{:S(2)}) async-start(), calls=%async_computation.8 | async-start | bytes 8912896 | tf_op jit(solution)/shard_map/all_gather | solution.py:191
  440.7 216.8 %reduce-scatter.6.cloned.1.call-start = ((), (), s32[]{:S(2)}) async-start(), calls=%async_computation.9 | async-start | bytes 2359296 | tf_op jit(solution)/shard_map/reduce_scatter | solution.py:198
  441.1 83.7 %copy-start.10 = (f32[16,64,1,128]{3,1,0,2:T(8,128)S(1)}, f32[16,64,1,128]{3,1,0,2:T(8,128)}, u32[]{:S(2)}) copy-start(f32[16,64,1,128]{3,1,0,2:T(8,128)} %get-tuple-element.411) | copy-start | bytes 1572868
  518.8 6.1 copy-start.3
  518.8 6.1 copy-start.14
  529.6 9.0 %copy-start.2 = (f32[16,64,1024]{2,1,0:T(8,128)}, f32[16,64,1024]{2,1,0:T(8,128)S(1)}, u32[]{:S(2)}) copy-start(f32[16,64,1024]{2,1,0:T(8,128)S(1)} %multiply_multiply_fusion) | copy-start | bytes 12582916
  584.1 106.7 %reduce-scatter.8.cloned.1.call-start = ((), (), s32[]{:S(2)}) async-start(), calls=%async_computation.10 | async-start | bytes 2359296 | tf_op jit(solution)/shard_map/reduce_scatter | solution.py:201
  645.9 4.1 copy-start.6
  650.0 42.6 %copy-start.1 = (bf16[256,4096]{1,0:T(8,128)(2,1)S(1)}, bf16[256,4096]{1,0:T(8,128)(2,1)}, u32[]{:S(2)}) copy-start(bf16[256,4096]{1,0:T(8,128)(2,1)} %param.17) | copy-start | bytes 6291460
Sparse Core Ops, SparseCore 0:
  9.7 44.3 all-gather.5
  55.7 40.3 all-gather.7
  98.3 52.0 all-gather.9
  152.4 51.3 all-gather.11
  243.3 197.3 reduce-scatter.3
  442.8 76.0 all-gather.13
  584.2 40.2 reduce-scatter.5
  650.1 40.6 reduce-scatter.7
where the time goes:
time: 701 us; the launch traced here: 699 us
  waiting for transfers between devices  341 us (49%)
  local copies, waits for them, and re-layouts  133 us (19%)
  other arithmetic  95.2 us (14%)
  matrix products  74.9 us (11%)
  blocking collectives  28.7 us (4%)
  between operations  14.4 us (2%)
  loops' own time  11.3 us (2%)
    reduce_scatter x1, waiting for transfers between devices, on_device(): lax.psum_scatter(partial_terms.astype(jnp.bfloat16), ('head', 'grp'), sca...  197 us
    gather x2, local copies, waits for them, and re-layouts, student_forward(): key_seg = segment_all[key_pos]  90.6 us
    all_gather x1, waiting for transfers between devices, on_device(): lax.all_gather(mismatch.astype(jnp.bfloat16), ('head', 'grp'), axis=1, ti...  77.8 us
    scatter-add x1, other arithmetic, student_backward(): value_total = jnp.zeros((token_count // BS, BS, width), jnp.float32).at[f...  39.1 us
    scatter-add x1, other arithmetic, student_backward(): key_total = jnp.zeros((token_count // BS, BS, width), jnp.float32).at[fla...  39 us
    all_gather x1, waiting for transfers between devices, on_device(): lax.all_gather(t_value, 'blk', axis=0, tiled=True)  32.4 us
    reduce_scatter x1, waiting for transfers between devices, on_device(): lax.psum_scatter(grad_values.astype(jnp.bfloat16), 'blk', scatter_dimensi...  31.6 us
    all_gather x1, blocking collectives, on_device(): lax.all_gather(segments, 'blk', axis=0, tiled=True)  28.7 us
  transfers between devices with their start and end apart: 8, of which 4 were waited for; matrix products, arithmetic and copies ran while one was open for 30% of the time, Pallas kernels for 0%

commit v1 on v0

--- a/solution.py
+++ b/solution.py
@@ -187,8 +187,16 @@
     mismatch = lax.psum_scatter(
         partial_terms.astype(jnp.bfloat16), ("head", "grp"), scatter_dimension=1, tiled=True
     ).astype(jnp.float32)
+
+    def sector_pass(array_here):
+        newest = lax.axis_size(("head", "grp"))
+        response = jnp.stack(newest * [array_here])
+        f_now = lax.all_to_all(response, ("head", "grp"), 0, 0)
+        b_now = jnp.concatenate(f_now, axis=1)
+        return b_now
+
     grad_attn = lax.dot_general(
-        lax.all_gather(mismatch.astype(jnp.bfloat16), ("head", "grp"), axis=1, tiled=True),
+        sector_pass(mismatch.astype(jnp.bfloat16)),
         s_out,
         contract,
         preferred_element_type=jnp.float32,

time: 701 us -> 763 us (1.088); the launches traced: 699 us -> 753 us
  local copies, waits for them, and re-layouts: 133 us -> 164 us
  waiting for transfers between devices: 341 us -> 359 us
    all_to_all x0 -> x1, waiting for transfers between devices: none -> 95.3 us  [sector_pass(): f_now = lax.all_to_all(response, ('head', 'grp'), 0, 0)]
    all_gather x1 -> x0, waiting for transfers between devices: 77.8 us -> none  [on_device(): lax.all_gather(mismatch.astype(jnp.bfloat16), ('head', 'grp'), axis=1, ti...]
    dot_general x0 -> x1, local copies, waits for them, and re-layouts: none -> 13.8 us  [on_device(): lax.dot_general(sector_pass(mismatch.astype(jnp.bfloat16)), s_out, contra...]
    reshape x0 -> x1, local copies, waits for them, and re-layouts: none -> 11.4 us  [sector_pass(): b_now = jnp.concatenate(f_now, axis=1)]
  transfers between devices with their start and end apart: 8 -> 8, of which waited for: 4 -> 4; matrix products, arithmetic and copies ran while one was open for 30% -> 28% of each run, Pallas kernels for 0% -> 0%
where the time goes in v1:
time: 763 us; the launch traced here: 753 us
  waiting for transfers between devices  359 us (47%)
  local copies, waits for them, and re-layouts  164 us (21%)
  other arithmetic  95 us (12%)
  matrix products  75.3 us (10%)
  blocking collectives  28.7 us (4%)
  between operations  14.6 us (2%)
  loops' own time  11.7 us (2%)
    reduce_scatter x1, waiting for transfers between devices, on_device(): lax.psum_scatter(partial_terms.astype(jnp.bfloat16), ('head', 'grp'), sca...  198 us
    all_to_all x1, waiting for transfers between devices, sector_pass(): f_now = lax.all_to_all(response, ('head', 'grp'), 0, 0)  95.3 us
    gather x2, local copies, waits for them, and re-layouts, student_forward(): key_seg = segment_all[key_pos]  90.6 us
    scatter-add x1, other arithmetic, student_backward(): value_total = jnp.zeros((token_count // BS, BS, width), jnp.float32).at[f...  39.1 us
    scatter-add x1, other arithmetic, student_backward(): key_total = jnp.zeros((token_count // BS, BS, width), jnp.float32).at[fla...  39 us
    reduce_scatter x1, waiting for transfers between devices, on_device(): lax.psum_scatter(grad_values.astype(jnp.bfloat16), 'blk', scatter_dimensi...  32.5 us
    all_gather x1, waiting for transfers between devices, on_device(): lax.all_gather(t_value, 'blk', axis=0, tiled=True)  32.4 us
    all_gather x1, blocking collectives, on_device(): lax.all_gather(segments, 'blk', axis=0, tiled=True)  28.7 us
  transfers between devices with their start and end apart: 8, of which 4 were waited for; matrix products, arithmetic and copies ran while one was open for 28% of the time, Pallas kernels for 0%

profile of v1, /device:TPU:0, one launch (start us, length us, event | category | flops | bytes accessed | tf_op | source)
XLA Modules:
  0.0 753.3 jit_solution(7252078792190482699)
XLA Ops:
  8.7 2.0 copy.27
  10.8 2.0 copy.29
  14.1 28.7 %all_gather.17 = s32[8192]{0:T(1024)S(1)} all-gather(s32[1024]{0:T(1024)S(1)} %copy-done.11), channel_id=1, replica_groups=mesh['blk'=8,'head'=8,'grp'=2] {'blk'}, dimensions={0}, use_global_device_ids=true | all-gather | bytes 36864 | tf_op jit(solution)/shard_map/all_gather | solution.py:171
  42.8 6.1 gather_fusion.2
  49.2 90.5 %gather_fusion.1 = s32[16384]{0:T(1024)S(1)} fusion(s32[8192]{0:T(1024)S(1)} %all_gather.17, s32[16384]{0:T(1024)S(1)} %broadcast_clamp_fusion), kind=kCustom, calls=%fused_computation.1 | custom fusion | bytes 196608 | tf_op jit(solution)/shard_map/gather | solution.py:28
  141.0 4.8 gather_fusion
  145.8 4.7 gather_fusion.3
  150.5 6.2 fusion.30
  156.7 6.7 fusion.31
  163.3 8.1 %fusion.32 = f32[1024,4096]{1,0:T(8,128)} fusion(bf16[1024,128]{1,0:T(8,128)(2,1)S(1)} %bitcast.106, bf16[128,4096]{1,0:T(8,128)(2,1)S(1)} %copy-done.7), kind=kOutput, calls=%fused_computation.63 | convolution fusion | flops 1073741824 | bytes 18087936 | tf_op jit(solution)/shard_map/dot_general | solution.py:183
  171.4 32.4 %all-gather.11.cloned.1.call-done = bf16[8192,256]{0,1:T(8,128)(2,1)} async-done(((bf16[1024,256]{0,1:T(8,128)(2,1)}), bf16[8192,256]{0,1:T(8,128)(2,1)}) %all-gather.11.cloned.1.call-update) | async-done | bytes 4194320 | tf_op jit(solution)/shard_map/all_gather | solution.py:162
  203.9 1.0 broadcast_in_dim.72
  204.9 25.6 %while.18 = (s32[]{:T(128)}, f32[2,1024]{1,0:T(2,128)S(1)}, f32[2,1024]{1,0:T(2,128)S(1)}, f32[2,1024,128]{2,1,0:T(8,128)}, s32[]{:T(128)}, /*index=5*/s32[8192]...) while((s32[]{:T(128)}, f32[2,1024]{1,0:T(2,128)S(1)}, ...), condition=%wide.region_7.8_spmd.clone, body=%wide.region_2.7_spmd.clone.sunk | while | flops 552605184 | bytes 27425168 | solution.py:142
  206.0 7.0 conditional.3
  206.6 1.1 constant_dynamic-slice_fusion
  207.7 1.1 fusion.2
  208.8 1.1 fusion.4
  210.0 2.0 fusion.8
  212.0 1.0 copy-done.5
  213.6 7.0 conditional.3
  214.2 1.1 constant_dynamic-slice_fusion
  215.3 1.1 fusion.2
  216.4 1.1 fusion.4
  217.6 2.0 fusion.8
  230.5 1.6 copy.31
  232.2 11.4 %subtract_convert_fusion = bf16[1024,4096]{1,0:T(8,128)(2,1)} fusion(f32[1024,4096]{1,0:T(8,128)} %fusion.32, bf16[1024,256]{0,1:T(8,128)(2,1)S(1)} %bitcast.103, bf16[256,4096]{1,0:T(8,128)(2,1)S(1)} %copy-done), kind=kOutput, calls=%fused_computation.26 | convolution fusion | flops 2155872256 | bytes 27787264 | tf_op jit(solution)/shard_map/dot_general | solution.py:183
  243.6 197.5 %reduce-scatter.4.cloned.1.call-done = bf16[1024,256]{1,0:T(8,128)(2,1)} async-done(((bf16[1024,4096]{1,0:T(8,128)(2,1)}), bf16[1024,256]{1,0:T(8,128)(2,1)}) %reduce-scatter.4.cloned.1.call-update) | async-done | bytes 524304 | tf_op jit(solution)/shard_map/reduce_scatter | solution.py:187
  441.1 5.1 stack.2
  446.2 4.9 all-to-all-start
  451.2 95.3 %all-to-all-done = bf16[16,1024,256]{2,1,0:T(8,128)(2,1)} async-done(((bf16[16,1024,256]{2,1,0:T(8,128)(2,1)}), bf16[16,1024,256]{2,1,0:T(8,128)(2,1)}, u32[]{:S(2)}, u32[]{:S(2)}) %all-to-all-start) | async-done | bytes 8388640 | tf_op jit(solution)/shard_map/all_to_all | solution.py:194
  546.5 11.4 %copy.32 = bf16[1024,16,256]{2,1,0:T(8,128)(2,1)} copy(bf16[1024,16,256]{2,0,1:T(8,128)(2,1)} %bitcast.16) | data formatting | bytes 16777216 | tf_op jit(solution)/shard_map/reshape | solution.py:195
  557.9 13.8 %dot_general.56 = bf16[16,64,4096]{2,1,0:T(8,128)(2,1)} reshape(bf16[1024,16,256]{2,1,0:T(8,128)(2,1)} %copy.32) | data formatting | bytes 16777216 | tf_op jit(solution)/shard_map/dot_general | solution.py:198
  571.7 5.9 fusion.24
  577.7 4.6 multiply_multiply_fusion
  582.3 9.0 %fusion.34 = f32[16,1024,128]{2,1,0:T(8,128)} fusion(f32[16,64,1024]{2,1,0:T(8,128)S(1)} %multiply_multiply_fusion, bf16[16,64,128]{2,1,0:T(8,128)(2,1)S(1)} %bitcast.108), kind=kOutput, calls=%fused_computation.65 | convolution fusion | flops 1610612736 | bytes 12845056 | tf_op jit(solution)/shard_map/bhqk,bqhd->bkhd/dot_general | solution.py:66
  591.2 2.5 broadcast.202.clone
  593.8 39.0 %scatter_fusion = f32[128,64,128]{2,1,0:T(8,128)} fusion(f32[128,64,128]{2,1,0:T(8,128)} %broadcast.202.clone, s32[256]{0:T(256)S(1)} %bitcast.110, f32[256,64,128]{2,1,0:T(8,128)} %bitcast.92), kind=kCustom, calls=%fused_computation.4 | custom fusion | flops 2097152 | bytes 25166848 | tf_op jit(solution)/shard_map/scatter-add | solution.py:77
  632.8 4.0 convert_element_type.63
  636.9 10.8 %convolution_bitcast_fusion = f32[16,1024,1,128]{1,3,0,2:T(8,128)} fusion(f32[16,64,128]{2,1,0:T(8,128)S(1)} %get-tuple-element.413, f32[16,64,1024]{2,1,0:T(8,128)} %get-tuple-element.409, f32[16,64]{1,0:T(8,128)S(1)} %get-tuple-element.408), kind=kOutput, calls=%fused_computation.31 | convolution fusion | flops 1611661312 | bytes 13111296 | tf_op jit(solution)/shard_map/bhqk,bqhd->bkhd/dot_general | solution.py:52
  647.7 9.3 %copy.33 = f32[16,1024,1,128]{3,1,0,2:T(8,128)} copy(f32[16,1024,1,128]{1,3,0,2:T(8,128)} %convolution_bitcast_fusion) | data formatting | bytes 16777216 | tf_op jit(solution)/shard_map/bhqk,bqhd->bkhd/transpose | solution.py:52
  657.0 2.5 broadcast.202.clone.1
  659.5 39.1 %scatter_fusion.1 = f32[128,64,128]{2,1,0:T(8,128)} fusion(f32[128,64,128]{2,1,0:T(8,128)} %broadcast.202.clone.1, s32[256]{0:T(256)S(1)} %bitcast.111, f32[256,64,128]{2,1,0:T(8,128)} %bitcast.91), kind=kCustom, calls=%fused_computation.5 | custom fusion | flops 2097152 | bytes 25166848 | tf_op jit(solution)/shard_map/scatter-add | solution.py:82
  698.6 4.1 convert_element_type.66
  702.7 1.0 convert_element_type.62
  703.8 6.4 fusion.33
  710.2 1.8 convert_element_type.65
  712.0 32.5 %reduce-scatter.8.cloned.1.call-done = bf16[1024,128]{1,0:T(8,128)(2,1)} async-done(((bf16[8192,128]{1,0:T(8,128)(2,1)}), bf16[1024,128]{1,0:T(8,128)(2,1)}) %reduce-scatter.8.cloned.1.call-update) | async-done | bytes 262160 | tf_op jit(solution)/shard_map/reduce_scatter | solution.py:209
  744.4 1.8 convert_element_type.68
  (150 shorter events, 7.3 us)
Async XLA Ops:
  7.2 225.0 %copy-start = (bf16[256,4096]{1,0:T(8,128)(2,1)S(1)}, bf16[256,4096]{1,0:T(8,128)(2,1)}, u32[]{:S(2)}) copy-start(bf16[256,4096]{1,0:T(8,128)(2,1)} %param.17) | copy-start | bytes 6291460
  7.2 6.9 copy-start.11
  7.2 133.8 %all-gather.5.cloned.1.call-start = ((), (), s32[]{:S(2)}) async-start(), calls=%async_computation.4 | async-start | bytes 2359296 | tf_op jit(solution)/shard_map/all_gather | solution.py:170
  7.9 137.8 %all-gather.7.cloned.1.call-start = ((), (), s32[]{:S(2)}) async-start(), calls=%async_computation.5 | async-start | bytes 2359296 | tf_op jit(solution)/shard_map/all_gather | solution.py:169
  8.7 162.7 %all-gather.9.cloned.1.call-start = ((), (), s32[]{:S(2)}) async-start(), calls=%async_computation.6 | async-start | bytes 4718592 | tf_op jit(solution)/shard_map/all_gather | solution.py:161
  10.8 193.1 %all-gather.11.cloned.1.call-start = ((), (), s32[]{:S(2)}) async-start(), calls=%async_computation.7 | async-start | bytes 4718592 | tf_op jit(solution)/shard_map/all_gather | solution.py:162
  12.9 428.2 %reduce-scatter.4.cloned.1.call-start = ((), (), s32[]{:S(2)}) async-start(), calls=%async_computation.8 | async-start | bytes 8912896 | tf_op jit(solution)/shard_map/reduce_scatter | solution.py:187
  49.2 91.2 %copy-start.9 = (bf16[1024,256]{1,0:T(8,128)(2,1)S(1)}, bf16[1024,256]{1,0:T(8,128)(2,1)}, u32[]{:S(2)}) copy-start(bf16[1024,256]{1,0:T(8,128)(2,1)} %param.14) | copy-start | bytes 1572868
  145.8 4.7 copy-start.10
  156.7 6.7 copy-start.7
  207.7 2.3 copy-start.4
  212.0 1.0 copy-start.5
  215.3 2.3 copy-start.4
  219.6 1.0 copy-start.5
  446.2 4.9 copy-start.12
  446.2 100.3 %all-to-all-start = ((bf16[16,1024,256]{2,1,0:T(8,128)(2,1)}), bf16[16,1024,256]{2,1,0:T(8,128)(2,1)}, u32[]{:S(2)}, u32[]{:S(2)}) async-start(bf16[16,1024,256]{2,1,0:T(8,128)(2,1)} %stack.2), calls=%async_computation.1 | async-start | bytes 16777216 | tf_op jit(solution)/shard_map/all_to_all | solution.py:194
  451.1 259.1 %reduce-scatter.6.cloned.1.call-start = ((), (), s32[]{:S(2)}) async-start(), calls=%async_computation.9 | async-start | bytes 2359296 | tf_op jit(solution)/shard_map/reduce_scatter | solution.py:206
  557.9 13.8 %copy-start.8 = (bf16[128,4096]{1,0:T(8,128)(2,1)S(1)}, bf16[128,4096]{1,0:T(8,128)(2,1)}, u32[]{:S(2)}) copy-start(bf16[128,4096]{1,0:T(8,128)(2,1)} %param.21) | copy-start | bytes 3145732
  557.9 13.8 %copy-start.14 = (f32[16,64,1,128]{3,1,0,2:T(8,128)S(1)}, f32[16,64,1,128]{3,1,0,2:T(8,128)}, u32[]{:S(2)}) copy-start(f32[16,64,1,128]{3,1,0,2:T(8,128)} %get-tuple-element.411) | copy-start | bytes 1572868
  571.7 6.0 copy-start.3
  571.7 6.0 copy-start.13
  582.3 9.0 %copy-start.2 = (f32[16,64,1024]{2,1,0:T(8,128)}, f32[16,64,1024]{2,1,0:T(8,128)S(1)}, u32[]{:S(2)}) copy-start(f32[16,64,1024]{2,1,0:T(8,128)S(1)} %multiply_multiply_fusion) | copy-start | bytes 12582916
  636.8 107.6 %reduce-scatter.8.cloned.1.call-start = ((), (), s32[]{:S(2)}) async-start(), calls=%async_computation.10 | async-start | bytes 2359296 | tf_op jit(solution)/shard_map/reduce_scatter | solution.py:209
  698.6 4.1 copy-start.6
  702.7 43.5 %copy-start.1 = (bf16[256,4096]{1,0:T(8,128)(2,1)S(1)}, bf16[256,4096]{1,0:T(8,128)(2,1)}, u32[]{:S(2)}) copy-start(bf16[256,4096]{1,0:T(8,128)(2,1)} %param.17) | copy-start | bytes 6291460
Sparse Core Ops, SparseCore 0:
  9.7 44.3 all-gather.4
  55.7 40.3 all-gather.6
  98.3 52.0 all-gather.8
  152.4 51.3 all-gather.10
  243.7 197.3 reduce-scatter.3
  636.9 41.3 reduce-scatter.5
  702.8 41.5 reduce-scatter.7
